TPU v7x, 512 devices: a whole 4x4x16 slice. The times are simulated.
512 devices in a mesh: tile: 128 (over z, x, core), layer: 4 (over y).
Axes of the slice: x: 4, y: 4, z: 16, core: 2. Of those that a mesh axis runs over, the one named last changes fastest.
Arguments:
- head_start: float32 [8, 8192, 512], P('layer', 'tile'), may hold values from -2 to 0.5
- soil_class: int32 [8, 8192, 512], P('layer', 'tile'), may hold values from 0 to 11
- land_mask: int32 [8192, 512], P('tile'), may hold values 0 or 1
- ks_table: float32 [12], replicated, may hold values from 0.2 to 5
- alpha_table: float32 [12], replicated, may hold values from 0.5 to 2
- store_table: float32 [12], replicated, may hold values from 0.5 to 2
- section: float32 [2048, 128], P('tile'), may hold values from -6 to 6
- cross_owner: int32 [128, 256], P('tile'), may hold values from 0 to 127, as said below
- cross_local: int32 [128, 256], P('tile'), may hold values from 0 to 15
- node_cell: int32 [128, 256, 128], P('tile'), may hold values from -1 to 32767, as said below
- bed_cond: float32 [128, 256, 128], P('tile'), may hold values from 0.5 to 4
Outputs:
- head: float32 [8, 8192, 512], P('layer', 'tile')
- inflow: float32 [2048, 128], P('tile', 'layer')
Inputs may be any that keep to these rules, and one draw needn't show every extreme that they name: `cross_owner`: no strip's row names one owner in more than 2 slots, and in every row some owner is named in exactly 2 slots. `node_cell`: -1 marks a node outside the strip; other values index the strip's top-layer cells row-major over 64 x 512. In each strip the slots with nodes come first, the rest are padding with every node -1.
All inputs are finite; a program needn't handle non-finite values. No bound on the sum of `land_mask` on one device may be relied on, other than what follows from the above.
Results may differ from a plain program's by a relative error of at most 0.00002.
Values sent between devices are 32-bit elements; how exact they have to be, the bound alone decides.
A program may use at most 64 MiB of HBM per device.

v0:
```python
import jax
import jax.numpy as jnp
from jax import lax
from jax.sharding import PartitionSpec as P

ITERS = 2
SWEEPS = 3
LATERAL = 1.0
VERTICAL = 2.0
GRAVITY = 1.0
NEIGHBOURS = (
    (0, -1, VERTICAL),
    (0, 1, VERTICAL),
    (1, -1, LATERAL),
    (1, 1, LATERAL),
    (2, -1, LATERAL),
    (2, 1, LATERAL),
)


def with_halo(block, sides, width):
    for axis, dim in sides:
        count = lax.axis_size(axis)
        forward = [(i, i + 1) for i in range(count - 1)]
        backward = [(target, source) for source, target in forward]
        low = lax.ppermute(
            lax.slice_in_dim(block, block.shape[dim] - width, None, axis=dim), axis, forward
        )
        high = lax.ppermute(lax.slice_in_dim(block, 0, width, axis=dim), axis, backward)
        block = jnp.concatenate([low, block, high], axis=dim)
    return block


def from_root(value, axis, source):
    kept = jnp.where(lax.axis_index(axis) == source, value, 0).astype(value.dtype)
    return lax.psum(kept, axis)


def beside(padded, axis_id, step):
    spans = [slice(1, -1), slice(1, -1), slice(1, -1)]
    spans[axis_id] = slice(1 + step, padded.shape[axis_id] - 1 + step)
    return padded[tuple(spans)]


def neighbor_weights(cond_pad, open_pad):
    centre = cond_pad[1:-1, 1:-1, 1:-1]
    centre_open = open_pad[1:-1, 1:-1, 1:-1]
    result = []
    for axis_id, step, factor in NEIGHBOURS:
        far = beside(cond_pad, axis_id, step)
        far_open = beside(open_pad, axis_id, step)
        result.append(factor * 2.0 * centre_open * far_open / (centre + far))
    return result


def relax(head_pad, weights, store, head_old, riv_diag, riv_rhs):
    total = store * head_old
    diagonal_sum = store
    for weight, (axis_id, step, factor) in zip(weights, NEIGHBOURS):
        total = total + weight * beside(head_pad, axis_id, step)
        diagonal_sum = diagonal_sum + weight
    total = total + GRAVITY * (weights[0] - weights[1]) + riv_rhs
    return total / (diagonal_sum + riv_diag)


def lookup(values_table, classes):
    result = jnp.zeros(classes.shape, jnp.float32)
    for class_id in range(values_table.shape[0]):
        result = jnp.where(classes == class_id, values_table[class_id], result)
    return result


def pad_dims(field, chosen_dims):
    widths = [(1, 1) if place in chosen_dims else (0, 0) for place in range(field.ndim)]
    return jnp.pad(field, widths)


def pick_heads(top_head, cells):
    breadth = top_head.shape[1]
    slots, width = cells.shape
    group = 16
    grouped = cells.reshape(slots // group, group * width)
    columns = jnp.arange(breadth, dtype=jnp.int32)[None, :]

    def one_group(flat_cells):
        picked_rows = jnp.take(top_head, flat_cells // breadth, axis=0)
        hit = columns == (flat_cells % breadth)[:, None]
        return jnp.sum(jnp.where(hit, picked_rows, 0.0), axis=1)

    return lax.map(one_group, grouped).reshape(slots, width)


def on_device(
    head_start,
    soil_class,
    land_mask,
    ks_table,
    alpha_table,
    store_table,
    section,
    cross_owner,
    cross_local,
    node_cell,
    bed_cond,
):
    layers, across, breadth = head_start.shape
    reach_rows = section.shape[0]
    node_count = section.shape[1]
    tile_count = lax.axis_size("tile")
    quarter = node_count // lax.axis_size("layer")
    node_first = lax.axis_index("layer") * quarter
    ks = lookup(ks_table, soil_class)
    alpha = lookup(alpha_table, soil_class)
    store = lookup(store_table, soil_class)
    landf = land_mask.astype(jnp.float32)[None]
    owners = cross_owner[0]
    positions = cross_local[0]
    node_cells = node_cell[0]
    bed_given = bed_cond[0]
    whole_section = lax.all_gather(section, "tile", axis=0, tiled=True)
    slot_section = jnp.take(whole_section, owners * reach_rows + positions, axis=0)
    in_tile = node_cells >= 0
    flat_index = jnp.where(in_tile, node_cells, across * breadth)
    bed_terms = jnp.where(in_tile, bed_given, 0.0)
    diag_top = (
        jnp.zeros((across * breadth,), jnp.float32)
        .at[flat_index.reshape(-1)]
        .add(bed_terms.reshape(-1), mode="drop")
    )
    rhs_top = (
        jnp.zeros((across * breadth,), jnp.float32)
        .at[flat_index.reshape(-1)]
        .add((bed_terms * slot_section).reshape(-1), mode="drop")
    )
    top_diag = diag_top.reshape(across, breadth)
    top_rhs = rhs_top.reshape(across, breadth)
    head_old, ks_here, alpha_here, store_here, land_here = (head_start, ks, alpha, store, landf)
    on_top = (lax.axis_index("layer") == 0).astype(jnp.float32)
    riv_diag = jnp.zeros((layers, across, breadth), jnp.float32).at[0].set(top_diag * on_top)
    riv_rhs = jnp.zeros((layers, across, breadth), jnp.float32).at[0].set(top_rhs * on_top)

    def head_halo(field):
        return pad_dims(with_halo(field, (("tile", 1), ("layer", 0)), 1), (2,))

    head = head_old
    for picard in range(ITERS):
        head_pad = head_halo(head)
        conduct = ks_here * jnp.exp(alpha_here * jnp.minimum(head, 0.0))
        both_pad = pad_dims(
            with_halo(jnp.stack([conduct, conduct * land_here]), (("tile", 2), ("layer", 1)), 1),
            (3,),
        )
        cond_pad = both_pad[0]
        open_pad = both_pad[1]
        weights = neighbor_weights(cond_pad, open_pad)
        for sweep in range(SWEEPS):
            if sweep > 0:
                head_pad = head_halo(head)
            head = relax(head_pad, weights, store_here, head_old, riv_diag, riv_rhs)
    top_head = from_root(head[0], "layer", 0)
    my_cells = lax.dynamic_slice_in_dim(node_cells, node_first, quarter, 1)
    my_bed = lax.dynamic_slice_in_dim(bed_given, node_first, quarter, 1)
    my_section = lax.dynamic_slice_in_dim(slot_section, node_first, quarter, 1)
    my_inside = my_cells >= 0
    node_head = pick_heads(top_head, jnp.where(my_inside, my_cells, 0))
    slot_in = jnp.where(my_inside, my_bed * (node_head - my_section), 0.0)
    dense = (
        jnp.zeros((reach_rows * tile_count, quarter), jnp.float32)
        .at[owners * reach_rows + positions]
        .add(slot_in)
    )
    inflow = lax.psum_scatter(dense, "tile", scatter_dimension=0, tiled=True)
    return (head, inflow)


def solution(mesh):
    placed = (
        P("layer", "tile", None),
        P("layer", "tile", None),
        P("tile", None),
        P(),
        P(),
        P(),
        P("tile", None),
        P("tile", None),
        P("tile", None),
        P("tile", None, None),
        P("tile", None, None),
    )
    return jax.shard_map(
        on_device,
        mesh=mesh,
        in_specs=placed,
        out_specs=(P("layer", "tile", None), P("tile", "layer")),
        check_vma=False,
    )
```

profile of v0, /device:TPU:8, one launch (start us, length us, event | category | flops | bytes accessed | tf_op | source)
XLA Modules:
  0.0 1032.4 jit_solution(11896485293692213495)
XLA Ops:
  7.2 1.8 fusion.137
  9.0 1.8 fusion.136
  11.7 17.8 %fusion.107 = (f32[1,2,64,512]{3,2,1,0:T(8,128)S(1)}, f32[2,64,512]{2,1,0:T(8,128)S(1)}, f32[2,64,512]{2,1,0:T(8,128)S(1)}, pred[2,64,512]{2,1,0:T(8,128)(4,1)S(...) fusion(f32[2,64,512]{2,1,0:T(8,128)} %param.17, ...), kind=kLoop, calls=%fused_computation.316 | loop fusion | flops 2555904 | bytes 2097248 | tf_op jit(solution)/shard_map/stack | solution.py:150
  31.0 3.0 collective-permute-start
  35.3 3.6 collective-permute-start.4
  40.6 7.1 collective-permute-start.7
  47.7 1.9 collective-permute-start.6
  49.8 3.9 collective-permute-start.3
  53.7 1.9 collective-permute-start.2
  56.7 4.8 collective-permute-done.3
  61.5 3.4 collective-permute-done.2
  66.5 8.5 add_add_fusion.1
  76.1 104.6 %all-gather.2.cloned.1.call-done = f32[2048,128]{1,0:T(8,128)} async-done(((f32[16,128]{1,0:T(8,128)}), f32[2048,128]{1,0:T(8,128)}) %all-gather.2.cloned.1.call-update) | async-done | bytes 1048592 | tf_op jit(solution)/shard_map/all_gather | solution.py:120
  180.6 1.9 gather_fusion.1
  182.6 1.7 bitcast_multiply_fusion.1
  184.3 171.3 %scatter_custom_fusion.1 = f32[32768]{0:T(1024)S(1)} fusion(s32[32768]{0:T(1024)} %bitcast.101, f32[32768]{0:T(1024)S(1)} %get-tuple-element.136, f32[]{:T(128)} %constant.189.clone.1), kind=kCustom, calls=%fused_computation.302 | custom fusion | flops 32768 | bytes 131584 | tf_op jit(solution)/shard_map/scatter-add | solution.py:128
  357.3 171.2 %scatter_custom_fusion = f32[32768]{0:T(1024)S(1)} fusion(s32[32768]{0:T(1024)} %bitcast.102, f32[32768]{0:T(1024)} %get-tuple-element.134, f32[]{:T(128)} %constant.189.clone.1), kind=kCustom, calls=%fused_computation.304 | custom fusion | flops 32768 | bytes 131584 | tf_op jit(solution)/shard_map/scatter-add | solution.py:133
  530.0 1.6 fusion.92
  534.0 3.0 collective-permute-start.8
  537.9 2.4 collective-permute-start.11
  540.3 3.4 collective-permute-start.10
  543.7 2.4 collective-permute-done.11
  546.1 2.7 collective-permute-done.10
  550.9 3.0 collective-permute-start.12
  554.8 1.9 collective-permute-start.15
  556.7 3.9 collective-permute-start.14
  560.6 2.0 collective-permute-done.15
  562.7 1.9 collective-permute-done.14
  567.5 3.1 collective-permute-start.20
  572.0 5.1 collective-permute-start.16
  578.0 1.9 collective-permute-start.19
  580.0 3.9 collective-permute-start.18
  583.9 1.9 collective-permute-start.23
  585.9 4.1 collective-permute-start.22
  590.0 2.6 collective-permute-done.23
  592.6 1.9 collective-permute-done.22
  598.7 3.0 collective-permute-start.24
  602.6 1.9 collective-permute-start.27
  604.6 3.9 collective-permute-start.26
  609.7 1.9 collective-permute-done.26
  613.7 4.8 collective-permute-start.28
  620.0 1.9 collective-permute-start.31
  621.9 3.9 collective-permute-start.30
  627.2 1.7 collective-permute-done.30
  630.5 75.9 %all-reduce.10.cloned.1.call-done = f32[64,512]{1,0:T(8,128)} async-done(((f32[64,512]{1,0:T(8,128)}), f32[64,512]{1,0:T(8,128)}) %all-reduce.10.cloned.1.call-update) | async-done | bytes 131088 | tf_op jit(solution)/shard_map/psum | solution.py:36
  706.4 54.5 %while.15 = (s32[]{:T(128)}, f32[16,512]{1,0:T(8,128)S(1)}, s32[16,512]{1,0:T(8,128)S(1)}, f32[64,512]{1,0:T(8,128)}, s32[]{:T(128)}, /*index=5*/s32[]{:T(128)}) while((s32[]{:T(128)}, f32[16,512]{1,0:T(8,128)S(1)}, s32[16,512]{1,0:T(8,128)S(1)}, f32[64,512]{1,0:T(8,128)}, s32[]{:T(128)}, /*index=5*/s32[]{:T(128)}) %tuple.130), condition=%wide.region_5.6_spmd.clone, body=%wide.region_3.5_spmd.clone.sunk | while | flops 1074690 | bytes 3175509 | solution.py:90
  706.4 3.0 gather_fusion
  709.9 2.9 gather_fusion
  713.3 2.9 gather_fusion
  716.7 2.9 gather_fusion
  720.1 2.9 gather_fusion
  723.5 2.9 gather_fusion
  726.9 2.9 gather_fusion
  730.3 2.9 gather_fusion
  733.7 2.9 gather_fusion
  737.1 2.9 gather_fusion
  740.5 2.9 gather_fusion
  743.9 2.9 gather_fusion
  747.3 2.9 gather_fusion
  750.7 2.9 gather_fusion
  754.1 2.9 gather_fusion
  757.5 2.9 gather_fusion
  761.0 2.6 scatter_custom_fusion.2
  763.6 262.3 %reduce-scatter.2.cloned.1.call-done = f32[16,32]{1,0:T(8,128)} async-done(((f32[2048,32]{1,0:T(8,128)}), f32[16,32]{1,0:T(8,128)}) %reduce-scatter.2.cloned.1.call-update) | async-done | bytes 2064 | tf_op jit(solution)/shard_map/reduce_scatter | solution.py:172
  (251 shorter events, 42.5 us)
Async XLA Ops:
  7.2 22.4 %copy-start = (f32[2,64,512]{2,1,0:T(8,128)S(1)}, f32[2,64,512]{2,1,0:T(8,128)}, u32[]{:S(2)}) copy-start(f32[2,64,512]{2,1,0:T(8,128)} %param.17) | copy-start | bytes 786436
  7.2 173.5 %all-gather.2.cloned.1.call-start = ((), (), s32[]{:S(2)}) async-start(), calls=%async_computation.1 | async-start | bytes 1056768 | tf_op jit(solution)/shard_map/all_gather | solution.py:120
  11.7 17.9 %copy-start.2 = (f32[64,512]{1,0:T(8,128)}, f32[64,512]{1,0:T(8,128)S(1)}, u32[]{:S(2)}) copy-start(f32[64,512]{1,0:T(8,128)S(1)} %convert_element_type.18) | copy-start | bytes 393220
  11.7 27.3 %copy-start.1 = (s32[1,256,128]{2,1,0:T(8,128)S(1)}, s32[1,256,128]{2,1,0:T(8,128)}, u32[]{:S(2)}) copy-start(s32[1,256,128]{2,1,0:T(8,128)} %param.26) | copy-start | bytes 393220
  29.6 10.4 %copy-start.22 = (s32[1,256]{1,0:T(1,128)S(1)}, s32[1,256]{1,0:T(1,128)}, u32[]{:S(2)}) copy-start(s32[1,256]{1,0:T(1,128)} %param.25) | copy-start | bytes 3076
  29.6 10.4 %copy-start.23 = (s32[1,256]{1,0:T(1,128)S(1)}, s32[1,256]{1,0:T(1,128)}, u32[]{:S(2)}) copy-start(s32[1,256]{1,0:T(1,128)} %param.24) | copy-start | bytes 3076
  29.7 19.9 %collective-permute-start.1 = (f32[2,2,1,512]{3,2,1,0:T(1,128)S(1)}, f32[2,2,1,512]{3,2,1,0:T(1,128)S(1)}, u32[]{:S(2)}, u32[]{:S(2)}) collective-permute-start(f32[2,2,1,512]{3,2,1,0:T(1,128)S(1)} %get-tuple-element.168), channel_id=1, source_target_pairs={{4,0},{8,4},{12,8},{16,12},{20,16},{24,20},{28,24},{32,28},{36,32}... | collective-permute-start | bytes 24584 | tf_op jit(solution)/shard_map/ppermute | solution.py:29
  31.0 18.6 %collective-permute-start = (f32[2,2,1,512]{3,2,1,0:T(1,128)S(1)}, f32[2,2,1,512]{3,2,1,0:T(1,128)S(1)}, u32[]{:S(2)}, u32[]{:S(2)}) collective-permute-start(f32[2,2,1,512]{3,2,1,0:T(1,128)S(1)} %get-tuple-element.167), channel_id=1, source_target_pairs={{0,4},{4,8},{8,12},{12,16},{16,20},{20,24},{24,28},{28,32},{32,36}... | collective-permute-start | bytes 24584 | tf_op jit(solution)/shard_map/ppermute | solution.py:26
  34.0 6.4 collective-permute-start.5
  35.3 5.1 collective-permute-start.4
  39.0 667.3 %all-reduce.10.cloned.1.call-start = ((), (), s32[]{:S(2)}) async-start(), calls=%async_computation.2 | async-start | bytes 262144 | tf_op jit(solution)/shard_map/psum | solution.py:36
  40.5 15.1 %copy-start.21 = (f32[12]{0:T(128)S(1)}, f32[12]{0:T(128)}, u32[]{:S(2)}) copy-start(f32[12]{0:T(128)} %param.22) | copy-start | bytes 148
  40.6 15.8 %collective-permute-start.7 = (f32[1,66,512]{2,1,0:T(8,128)S(1)}, f32[1,66,512]{2,1,0:T(8,128)S(1)}, u32[]{:S(2)}, u32[]{:S(2)}) collective-permute-start(f32[1,66,512]{2,1,0:T(8,128)S(1)} %get-tuple-element.180), channel_id=1, source_target_pairs={{1,0},{2,1},{3,2},{5,4},{6,5},{7,6},{9,8},{10,9},{11,10},{13,12},{... | collective-permute-start | bytes 405512 | tf_op jit(solution)/shard_map/ppermute | solution.py:29
  47.7 8.7 collective-permute-start.6
  49.8 11.8 %collective-permute-start.3 = (f32[2,1,66,512]{3,2,1,0:T(8,128)S(1)}, f32[2,1,66,512]{3,2,1,0:T(8,128)S(1)}, u32[]{:S(2)}, u32[]{:S(2)}) collective-permute-start(f32[2,1,66,512]{3,2,1,0:T(8,128)S(1)} %get-tuple-element.164), channel_id=1, source_target_pairs={{1,0},{2,1},{3,2},{5,4},{6,5},{7,6},{9,8},{10,9},{11,10},{13,12},{... | collective-permute-start | bytes 811016 | tf_op jit(solution)/shard_map/ppermute | solution.py:29
  53.7 11.2 %collective-permute-start.2 = (f32[2,1,66,512]{3,2,1,0:T(8,128)S(1)}, f32[2,1,66,512]{3,2,1,0:T(8,128)S(1)}, u32[]{:S(2)}, u32[]{:S(2)}) collective-permute-start(f32[2,1,66,512]{3,2,1,0:T(8,128)S(1)} %get-tuple-element.163), channel_id=1, source_target_pairs={{0,1},{1,2},{2,3},{4,5},{5,6},{6,7},{8,9},{9,10},{10,11},{12,13},{... | collective-permute-start | bytes 811016 | tf_op jit(solution)/shard_map/ppermute | solution.py:26
  56.4 9.1 copy-start.6
  56.4 9.0 copy-start.8
  65.5 0.8 copy-start.13
  65.5 0.9 copy-start.14
  65.5 0.9 copy-start.15
  65.5 0.9 copy-start.16
  65.5 0.9 copy-start.17
  65.5 1.0 copy-start.18
  65.5 1.0 copy-start.19
  65.5 1.0 copy-start.20
  66.5 8.5 copy-start.7
  66.5 8.5 copy-start.9
  357.3 180.6 %copy-start.4 = (f32[1,64,512]{2,1,0:T(8,128)}, f32[1,64,512]{2,1,0:T(8,128)S(1)}, u32[]{:S(2)}) copy-start(f32[1,64,512]{2,1,0:T(8,128)S(1)} %mul.274) | copy-start | bytes 393220
  532.7 4.3 collective-permute-start.9
  534.0 3.8 collective-permute-start.8
  537.9 8.2 collective-permute-start.11
  540.3 8.4 collective-permute-start.10
  549.5 4.3 collective-permute-start.13
  550.9 3.8 collective-permute-start.12
  554.8 7.9 collective-permute-start.15
  556.7 7.9 collective-permute-start.14
  565.2 0.9 copy-start.3
  566.2 10.9 %collective-permute-start.21 = (f32[2,1,512]{2,1,0:T(1,128)S(1)}, f32[2,1,512]{2,1,0:T(1,128)S(1)}, u32[]{:S(2)}, u32[]{:S(2)}) collective-permute-start(f32[2,1,512]{2,1,0:T(1,128)S(1)} %get-tuple-element.186), channel_id=1, source_target_pairs={{4,0},{8,4},{12,8},{16,12},{20,16},{24,20},{28,24},{32,28},{36,32}... | collective-permute-start | bytes 12296 | tf_op jit(solution)/shard_map/ppermute | solution.py:29
  567.5 9.6 collective-permute-start.20
  570.7 6.5 collective-permute-start.17
  572.0 6.0 collective-permute-start.16
  578.0 16.8 %collective-permute-start.19 = (f32[2,1,66,512]{3,2,1,0:T(8,128)S(1)}, f32[2,1,66,512]{3,2,1,0:T(8,128)S(1)}, u32[]{:S(2)}, u32[]{:S(2)}) collective-permute-start(f32[2,1,66,512]{3,2,1,0:T(8,128)S(1)} %get-tuple-element.162), channel_id=1, source_target_pairs={{1,0},{2,1},{3,2},{5,4},{6,5},{7,6},{9,8},{10,9},{11,10},{13,12},{... | collective-permute-start | bytes 811016 | tf_op jit(solution)/shard_map/ppermute | solution.py:29
  580.0 14.9 %collective-permute-start.18 = (f32[2,1,66,512]{3,2,1,0:T(8,128)S(1)}, f32[2,1,66,512]{3,2,1,0:T(8,128)S(1)}, u32[]{:S(2)}, u32[]{:S(2)}) collective-permute-start(f32[2,1,66,512]{3,2,1,0:T(8,128)S(1)} %get-tuple-element.161), channel_id=1, source_target_pairs={{0,1},{1,2},{2,3},{4,5},{5,6},{6,7},{8,9},{9,10},{10,11},{12,13},{... | collective-permute-start | bytes 811016 | tf_op jit(solution)/shard_map/ppermute | solution.py:26
  583.9 8.7 collective-permute-start.23
  585.9 8.7 collective-permute-start.22
  596.4 0.9 copy-start.5
  597.4 4.3 collective-permute-start.25
  598.7 3.8 collective-permute-start.24
  602.6 7.0 collective-permute-start.27
  604.6 7.0 collective-permute-start.26
  612.4 6.1 collective-permute-start.29
  613.7 5.6 collective-permute-start.28
  620.0 7.2 collective-permute-start.31
  621.9 7.0 collective-permute-start.30
  629.7 76.7 %copy-start.10 = (f32[2,64,512]{2,1,0:T(8,128)}, f32[2,64,512]{2,1,0:T(8,128)S(1)}, u32[]{:S(2)}) copy-start(f32[2,64,512]{2,1,0:T(8,128)S(1)} %div.91) | copy-start | bytes 786436
  630.4 395.5 %reduce-scatter.2.cloned.1.call-start = ((), (), s32[]{:S(2)}) async-start(), calls=%async_computation.3 | async-start | bytes 1056768 | tf_op jit(solution)/shard_map/reduce_scatter | solution.py:172
  706.4 54.6 %copy-start.11 = (f32[1,256,128]{2,1,0:T(8,128)S(1)}, f32[1,256,128]{2,1,0:T(8,128)}, u32[]{:S(2)}) copy-start(f32[1,256,128]{2,1,0:T(8,128)} %param.27) | copy-start | bytes 393220
  706.4 54.6 %copy-start.12 = (f32[256,128]{1,0:T(8,128)S(1)}, f32[256,128]{1,0:T(8,128)}, u32[]{:S(2)}) copy-start(f32[256,128]{1,0:T(8,128)} %get-tuple-element.135) | copy-start | bytes 393220
Sparse Core Ops, SparseCore 0:
  39.1 141.4 all-gather.1
  630.6 75.7 all-reduce.9
  763.7 262.1 reduce-scatter.1
where the time goes:
time: 1030 us
  waiting for transfers between devices  475 us (46%)
  other arithmetic  393 us (38%)
  starting transfers between devices  89.4 us (9%)
  local copies, waits for them, and re-layouts  59.6 us (6%)
  between operations  14.7 us (1%)
    reduce_scatter x1, waiting for transfers between devices, on_device(): inflow = lax.psum_scatter(dense, 'tile', scatter_dimension=0, tiled=True)  262 us
    scatter-add x1, other arithmetic, on_device(): diag_top = jnp.zeros((across * breadth,), jnp.float32).at[flat_index.resh...  171 us
    scatter-add x1, other arithmetic, on_device(): rhs_top = jnp.zeros((across * breadth,), jnp.float32).at[flat_index.resha...  171 us
    all_gather x1, waiting for transfers between devices, on_device(): whole_section = lax.all_gather(section, 'tile', axis=0, tiled=True)  105 us
    psum x1, waiting for transfers between devices, from_root(): return lax.psum(kept, axis)  75.9 us
    ppermute x16, starting transfers between devices, with_halo(): lax.ppermute(lax.slice_in_dim(block, block.shape[dim] - width, None, axis...  55.8 us
    gather x16, local copies, waits for them, and re-layouts, one_group(): picked_rows = jnp.take(top_head, flat_cells // breadth, axis=0)  47 us
    ppermute x16, starting transfers between devices, with_halo(): lax.ppermute(lax.slice_in_dim(block, 0, width, axis=dim), axis, backward)  33.4 us
  transfers between devices with their start and end apart: 35, of which 20 were waited for; matrix products, arithmetic and copies ran while one was open for 1% of the time, Pallas kernels for 0%

commit v1 on v0

--- a/solution.py
+++ b/solution.py
@@ -117,7 +117,9 @@
     positions = cross_local[0]
     node_cells = node_cell[0]
     bed_given = bed_cond[0]
-    whole_section = lax.all_gather(section, "tile", axis=0, tiled=True)
+    whole_section = jnp.concatenate(
+        lax.all_to_all(jnp.stack([section] * lax.axis_size("tile")), "tile", 0, 0), axis=0
+    )
     slot_section = jnp.take(whole_section, owners * reach_rows + positions, axis=0)
     in_tile = node_cells >= 0
     flat_index = jnp.where(in_tile, node_cells, across * breadth)

time: 1030 us -> 966 us (0.938)
  waiting for transfers between devices: 475 us -> 391 us
  starting transfers between devices: 89.4 us -> 107 us
    all_gather x1 -> x0, waiting for transfers between devices: 105 us -> none  [on_device(): whole_section = lax.all_gather(section, 'tile', axis=0, tiled=True)]
    all_to_all x0 -> x1, starting transfers between devices: none -> 26.5 us  [on_device(): lax.all_to_all(jnp.stack([section] * lax.axis_size('tile')), 'tile', 0, 0)]
    all_to_all x0 -> x1, waiting for transfers between devices: none -> 19.9 us  [on_device(): lax.all_to_all(jnp.stack([section] * lax.axis_size('tile')), 'tile', 0, 0)]
    ppermute x16, waiting for transfers between devices: 14.3 us -> 31.9 us  [with_halo(): lax.ppermute(lax.slice_in_dim(block, 0, width, axis=dim), axis, backward)]
    ppermute x16, starting transfers between devices: 55.8 us -> 44.7 us  [with_halo(): lax.ppermute(lax.slice_in_dim(block, block.shape[dim] - width, None, axis...]
  transfers between devices with their start and end apart: 35 -> 35, of which waited for: 20 -> 20; matrix products, arithmetic and copies ran while one was open for 1% -> 2% of each run, Pallas kernels for 0% -> 0%
where the time goes in v1:
time: 966 us; the launch traced here: 965 us
  waiting for transfers between devices  391 us (40%)
  other arithmetic  389 us (40%)
  starting transfers between devices  107 us (11%)
  local copies, waits for them, and re-layouts  60.7 us (6%)
  between operations  15.2 us (2%)
    reduce_scatter x1, waiting for transfers between devices, on_device(): inflow = lax.psum_scatter(dense, 'tile', scatter_dimension=0, tiled=True)  262 us
    scatter-add x1, other arithmetic, on_device(): diag_top = jnp.zeros((across * breadth,), jnp.float32).at[flat_index.resh...  171 us
    scatter-add x1, other arithmetic, on_device(): rhs_top = jnp.zeros((across * breadth,), jnp.float32).at[flat_index.resha...  171 us
    psum x1, waiting for transfers between devices, from_root(): return lax.psum(kept, axis)  66.4 us
    gather x16, local copies, waits for them, and re-layouts, one_group(): picked_rows = jnp.take(top_head, flat_cells // breadth, axis=0)  47 us
    ppermute x16, starting transfers between devices, with_halo(): lax.ppermute(lax.slice_in_dim(block, block.shape[dim] - width, None, axis...  44.7 us
    ppermute x16, starting transfers between devices, with_halo(): lax.ppermute(lax.slice_in_dim(block, 0, width, axis=dim), axis, backward)  36.1 us
    ppermute x16, waiting for transfers between devices, with_halo(): lax.ppermute(lax.slice_in_dim(block, 0, width, axis=dim), axis, backward)  31.9 us
  transfers between devices with their start and end apart: 35, of which 20 were waited for; matrix products, arithmetic and copies ran while one was open for 2% of the time, Pallas kernels for 0%

profile of v1, /device:TPU:8, one launch (start us, length us, event | category | flops | bytes accessed | tf_op | source)
XLA Modules:
  0.0 964.5 jit_solution(10779992966647085774)
XLA Ops:
  7.2 1.8 fusion.136
  9.0 1.8 fusion.137
  11.7 17.3 %fusion.107 = (f32[1,2,64,512]{3,2,1,0:T(8,128)S(1)}, f32[2,64,512]{2,1,0:T(8,128)S(1)}, f32[2,64,512]{2,1,0:T(8,128)S(1)}, pred[2,64,512]{2,1,0:T(8,128)(4,1)},...) fusion(f32[2,64,512]{2,1,0:T(8,128)} %param.17, ...), kind=kLoop, calls=%fused_computation.316 | loop fusion | flops 2555904 | bytes 2097248 | tf_op jit(solution)/shard_map/stack | solution.py:152
  29.8 1.7 collective-permute-start
  32.9 4.3 collective-permute-start.4
  39.7 26.5 %all-to-all-start = ((f32[128,16,128]{2,1,0:T(8,128)}), f32[128,16,128]{2,1,0:T(8,128)S(1)}, u32[]{:S(2)}, u32[]{:S(2)}) async-start(f32[128,16,128]{2,1,0:T(8,128)} %stack.17), calls=%async_computation | async-start | bytes 2097152 | tf_op jit(solution)/shard_map/all_to_all | solution.py:121
  68.4 3.5 collective-permute-start.6
  71.9 2.4 collective-permute-start.7
  74.4 3.5 collective-permute-start.2
  77.9 2.4 collective-permute-start.3
  81.3 2.9 collective-permute-done.2
  84.3 3.2 collective-permute-done.3
  89.2 8.6 add_add_fusion.1
  99.7 19.9 %all-to-all-done = f32[128,16,128]{2,1,0:T(8,128)S(1)} async-done(((f32[128,16,128]{2,1,0:T(8,128)}), f32[128,16,128]{2,1,0:T(8,128)S(1)}, u32[]{:S(2)}, u32[]{:S(2)}) %all-to-all-start) | async-done | bytes 1048608 | tf_op jit(solution)/shard_map/all_to_all | solution.py:121
  122.0 171.3 %scatter_custom_fusion = f32[32768]{0:T(1024)S(1)} fusion(s32[32768]{0:T(1024)} %bitcast.103, f32[32768]{0:T(1024)S(1)} %get-tuple-element.134, f32[]{:T(128)} %constant.189.clone.1), kind=kCustom, calls=%fused_computation.304 | custom fusion | flops 32768 | bytes 131584 | tf_op jit(solution)/shard_map/scatter-add | solution.py:135
  293.4 171.3 %scatter_custom_fusion.1 = f32[32768]{0:T(1024)S(1)} fusion(s32[32768]{0:T(1024)} %bitcast.104, f32[32768]{0:T(1024)S(1)} %get-tuple-element.136, f32[]{:T(128)} %constant.189.clone.1), kind=kCustom, calls=%fused_computation.302 | custom fusion | flops 32768 | bytes 131584 | tf_op jit(solution)/shard_map/scatter-add | solution.py:130
  467.6 2.2 collective-permute-done.9
  469.9 3.5 collective-permute-start.10
  473.4 2.4 collective-permute-start.11
  476.9 3.6 collective-permute-done.11
  481.3 3.2 collective-permute-start.12
  485.8 3.4 collective-permute-done.13
  489.2 3.2 collective-permute-start.14
  492.4 2.8 collective-permute-start.15
  496.4 3.5 collective-permute-done.15
  501.6 2.9 collective-permute-start.20
  505.8 4.6 collective-permute-start.16
  511.8 2.9 collective-permute-done.17
  514.9 1.9 collective-permute-start.18
  516.8 3.9 collective-permute-start.19
  520.8 1.9 collective-permute-start.22
  522.7 3.9 collective-permute-start.23
  526.7 2.7 collective-permute-done.22
  529.4 1.9 collective-permute-done.23
  535.0 2.2 collective-permute-start.24
  538.5 3.6 collective-permute-done.25
  542.1 1.9 collective-permute-start.26
  544.1 3.9 collective-permute-start.27
  549.3 1.9 collective-permute-done.27
  552.0 3.2 collective-permute-start.28
  556.5 4.0 collective-permute-done.29
  561.2 1.9 collective-permute-start.30
  563.1 3.9 collective-permute-start.31
  568.5 1.7 collective-permute-done.31
  571.8 66.4 %all-reduce.10.cloned.1.call-done = f32[64,512]{1,0:T(8,128)} async-done(((f32[64,512]{1,0:T(8,128)}), f32[64,512]{1,0:T(8,128)}) %all-reduce.10.cloned.1.call-update) | async-done | bytes 131088 | tf_op jit(solution)/shard_map/psum | solution.py:36
  638.2 54.5 %while.15 = (s32[]{:T(128)}, f32[16,512]{1,0:T(8,128)S(1)}, s32[16,512]{1,0:T(8,128)S(1)}, f32[64,512]{1,0:T(8,128)}, s32[]{:T(128)}, /*index=5*/s32[]{:T(128)}) while((s32[]{:T(128)}, f32[16,512]{1,0:T(8,128)S(1)}, s32[16,512]{1,0:T(8,128)S(1)}, f32[64,512]{1,0:T(8,128)}, s32[]{:T(128)}, /*index=5*/s32[]{:T(128)}) %tuple.130), condition=%wide.region_5.6_spmd.clone, body=%wide.region_3.5_spmd.clone.sunk | while | flops 1074690 | bytes 3175501 | solution.py:90
  638.2 3.0 gather_fusion
  641.7 2.9 gather_fusion
  645.1 2.9 gather_fusion
  648.5 2.9 gather_fusion
  651.9 2.9 gather_fusion
  655.3 2.9 gather_fusion
  658.7 2.9 gather_fusion
  662.1 2.9 gather_fusion
  665.5 2.9 gather_fusion
  668.9 2.9 gather_fusion
  672.3 2.9 gather_fusion
  675.7 2.9 gather_fusion
  679.1 2.9 gather_fusion
  682.5 2.9 gather_fusion
  685.9 2.9 gather_fusion
  689.3 2.9 gather_fusion
  692.8 2.6 scatter_custom_fusion.2
  695.4 262.3 %reduce-scatter.2.cloned.1.call-done = f32[16,32]{1,0:T(8,128)} async-done(((f32[2048,32]{1,0:T(8,128)}), f32[16,32]{1,0:T(8,128)}) %reduce-scatter.2.cloned.1.call-update) | async-done | bytes 2064 | tf_op jit(solution)/shard_map/reduce_scatter | solution.py:174
  (277 shorter events, 45.1 us)
Async XLA Ops:
  7.2 22.5 %copy-start = (f32[2,64,512]{2,1,0:T(8,128)S(1)}, f32[2,64,512]{2,1,0:T(8,128)}, u32[]{:S(2)}) copy-start(f32[2,64,512]{2,1,0:T(8,128)} %param.17) | copy-start | bytes 786436
  11.7 18.1 %copy-start.10 = (f32[64,512]{1,0:T(8,128)}, f32[64,512]{1,0:T(8,128)S(1)}, u32[]{:S(2)}) copy-start(f32[64,512]{1,0:T(8,128)S(1)} %convert_element_type.18) | copy-start | bytes 393220
  11.7 27.0 %copy-start.34 = (f32[16,128]{1,0:T(8,128)S(1)}, f32[16,128]{1,0:T(8,128)}, u32[]{:S(2)}) copy-start(f32[16,128]{1,0:T(8,128)} %param.23) | copy-start | bytes 24580
  29.8 44.4 %collective-permute-start = (f32[2,2,1,512]{3,2,1,0:T(1,128)S(1)}, f32[2,2,1,512]{3,2,1,0:T(1,128)S(1)}, u32[]{:S(2)}, u32[]{:S(2)}) collective-permute-start(f32[2,2,1,512]{3,2,1,0:T(1,128)S(1)} %get-tuple-element.167), channel_id=1, source_target_pairs={{0,4},{4,8},{8,12},{12,16},{16,20},{20,24},{24,28},{28,32},{32,36}... | collective-permute-start | bytes 24584 | tf_op jit(solution)/shard_map/ppermute | solution.py:26
  31.6 42.7 %collective-permute-start.1 = (f32[2,2,1,512]{3,2,1,0:T(1,128)S(1)}, f32[2,2,1,512]{3,2,1,0:T(1,128)S(1)}, u32[]{:S(2)}, u32[]{:S(2)}) collective-permute-start(f32[2,2,1,512]{3,2,1,0:T(1,128)S(1)} %get-tuple-element.168), channel_id=1, source_target_pairs={{4,0},{8,4},{12,8},{16,12},{20,16},{24,20},{28,24},{32,28},{36,32}... | collective-permute-start | bytes 24584 | tf_op jit(solution)/shard_map/ppermute | solution.py:29
  32.9 34.7 %collective-permute-start.4 = (f32[2,1,512]{2,1,0:T(1,128)S(1)}, f32[2,1,512]{2,1,0:T(1,128)S(1)}, u32[]{:S(2)}, u32[]{:S(2)}) collective-permute-start(f32[2,1,512]{2,1,0:T(1,128)S(1)} %get-tuple-element.191), channel_id=1, source_target_pairs={{0,4},{4,8},{8,12},{12,16},{16,20},{20,24},{24,28},{28,32},{32,36}... | collective-permute-start | bytes 12296 | tf_op jit(solution)/shard_map/ppermute | solution.py:26
  37.2 29.0 %copy-start.8 = (s32[1,256,128]{2,1,0:T(8,128)S(1)}, s32[1,256,128]{2,1,0:T(8,128)}, u32[]{:S(2)}) copy-start(s32[1,256,128]{2,1,0:T(8,128)} %param.26) | copy-start | bytes 393220
  37.2 29.9 %copy-start.35 = (s32[1,256]{1,0:T(1,128)S(1)}, s32[1,256]{1,0:T(1,128)}, u32[]{:S(2)}) copy-start(s32[1,256]{1,0:T(1,128)} %param.25) | copy-start | bytes 3076
  37.2 29.9 %copy-start.36 = (s32[1,256]{1,0:T(1,128)S(1)}, s32[1,256]{1,0:T(1,128)}, u32[]{:S(2)}) copy-start(s32[1,256]{1,0:T(1,128)} %param.24) | copy-start | bytes 3076
  37.2 30.4 %collective-permute-start.5 = (f32[2,1,512]{2,1,0:T(1,128)S(1)}, f32[2,1,512]{2,1,0:T(1,128)S(1)}, u32[]{:S(2)}, u32[]{:S(2)}) collective-permute-start(f32[2,1,512]{2,1,0:T(1,128)S(1)} %get-tuple-element.192), channel_id=1, source_target_pairs={{4,0},{8,4},{12,8},{16,12},{20,16},{24,20},{28,24},{32,28},{36,32}... | collective-permute-start | bytes 12296 | tf_op jit(solution)/shard_map/ppermute | solution.py:29
  39.7 79.9 %all-to-all-start = ((f32[128,16,128]{2,1,0:T(8,128)}), f32[128,16,128]{2,1,0:T(8,128)S(1)}, u32[]{:S(2)}, u32[]{:S(2)}) async-start(f32[128,16,128]{2,1,0:T(8,128)} %stack.17), calls=%async_computation | async-start | bytes 2097152 | tf_op jit(solution)/shard_map/all_to_all | solution.py:121
  66.2 572.0 %all-reduce.10.cloned.1.call-start = ((), (), s32[]{:S(2)}) async-start(), calls=%async_computation.2 | async-start | bytes 262144 | tf_op jit(solution)/shard_map/psum | solution.py:36
  67.7 12.6 %copy-start.33 = (f32[12]{0:T(128)S(1)}, f32[12]{0:T(128)}, u32[]{:S(2)}) copy-start(f32[12]{0:T(128)} %param.22) | copy-start | bytes 148
  68.4 12.6 %collective-permute-start.6 = (f32[1,66,512]{2,1,0:T(8,128)}, f32[1,66,512]{2,1,0:T(8,128)S(1)}, u32[]{:S(2)}, u32[]{:S(2)}) collective-permute-start(f32[1,66,512]{2,1,0:T(8,128)} %get-tuple-element.179), channel_id=1, source_target_pairs={{0,1},{1,2},{2,3},{4,5},{5,6},{6,7},{8,9},{9,10},{10,11},{12,13},{... | collective-permute-start | bytes 405512 | tf_op jit(solution)/shard_map/ppermute | solution.py:26
  71.9 9.1 collective-permute-start.7
  74.4 9.9 %collective-permute-start.2 = (f32[2,1,66,512]{3,2,1,0:T(8,128)S(1)}, f32[2,1,66,512]{3,2,1,0:T(8,128)S(1)}, u32[]{:S(2)}, u32[]{:S(2)}) collective-permute-start(f32[2,1,66,512]{3,2,1,0:T(8,128)S(1)} %get-tuple-element.163), channel_id=1, source_target_pairs={{0,1},{1,2},{2,3},{4,5},{5,6},{6,7},{8,9},{9,10},{10,11},{12,13},{... | collective-permute-start | bytes 811016 | tf_op jit(solution)/shard_map/ppermute | solution.py:26
  77.9 9.6 collective-permute-start.3
  81.0 7.0 copy-start.14
  81.0 7.0 copy-start.16
  88.0 0.9 copy-start.25
  88.0 1.0 copy-start.26
  88.1 1.0 copy-start.27
  88.1 1.0 copy-start.28
  88.1 1.0 copy-start.29
  88.1 1.0 copy-start.30
  88.1 1.1 copy-start.31
  88.1 1.1 copy-start.32
  89.2 9.3 copy-start.15
  89.2 9.3 copy-start.17
  120.3 344.5 %copy-start.9 = (f32[2,64,512]{2,1,0:T(8,128)S(1)}, f32[2,64,512]{2,1,0:T(8,128)}, u32[]{:S(2)}) copy-start(f32[2,64,512]{2,1,0:T(8,128)} %get-tuple-element.139) | copy-start | bytes 786436
  464.8 16.0 %copy-start.12 = (f32[1,64,512]{2,1,0:T(8,128)}, f32[1,64,512]{2,1,0:T(8,128)S(1)}, u32[]{:S(2)}) copy-start(f32[1,64,512]{2,1,0:T(8,128)S(1)} %mul.274) | copy-start | bytes 393220
  464.9 15.9 %copy-start.7 = (f32[2,64,512]{2,1,0:T(8,128)S(1)}, f32[2,64,512]{2,1,0:T(8,128)}, u32[]{:S(2)}) copy-start(f32[2,64,512]{2,1,0:T(8,128)} %get-tuple-element.141) | copy-start | bytes 786436
  465.0 2.6 collective-permute-start.8
  466.3 3.5 collective-permute-start.9
  469.9 7.0 collective-permute-start.10
  473.4 7.1 collective-permute-start.11
  481.3 4.5 collective-permute-start.12
  484.5 4.7 collective-permute-start.13
  489.2 7.2 collective-permute-start.14
  492.4 7.5 collective-permute-start.15
  500.2 1.0 copy-start.2
  500.2 1.0 copy-start.4
  500.6 0.9 copy-start.11
  501.6 10.1 %collective-permute-start.20 = (f32[2,1,512]{2,1,0:T(1,128)S(1)}, f32[2,1,512]{2,1,0:T(1,128)S(1)}, u32[]{:S(2)}, u32[]{:S(2)}) collective-permute-start(f32[2,1,512]{2,1,0:T(1,128)S(1)} %get-tuple-element.185), channel_id=1, source_target_pairs={{0,4},{4,8},{8,12},{12,16},{16,20},{20,24},{24,28},{28,32},{32,36}... | collective-permute-start | bytes 12296 | tf_op jit(solution)/shard_map/ppermute | solution.py:26
  504.5 7.3 collective-permute-start.21
  505.8 6.0 collective-permute-start.16
  510.5 4.3 collective-permute-start.17
  514.9 16.7 %collective-permute-start.18 = (f32[2,1,66,512]{3,2,1,0:T(8,128)S(1)}, f32[2,1,66,512]{3,2,1,0:T(8,128)S(1)}, u32[]{:S(2)}, u32[]{:S(2)}) collective-permute-start(f32[2,1,66,512]{3,2,1,0:T(8,128)S(1)} %get-tuple-element.161), channel_id=1, source_target_pairs={{0,1},{1,2},{2,3},{4,5},{5,6},{6,7},{8,9},{9,10},{10,11},{12,13},{... | collective-permute-start | bytes 811016 | tf_op jit(solution)/shard_map/ppermute | solution.py:26
  516.8 14.8 %collective-permute-start.19 = (f32[2,1,66,512]{3,2,1,0:T(8,128)S(1)}, f32[2,1,66,512]{3,2,1,0:T(8,128)S(1)}, u32[]{:S(2)}, u32[]{:S(2)}) collective-permute-start(f32[2,1,66,512]{3,2,1,0:T(8,128)S(1)} %get-tuple-element.162), channel_id=1, source_target_pairs={{1,0},{2,1},{3,2},{5,4},{6,5},{7,6},{9,8},{10,9},{11,10},{13,12},{... | collective-permute-start | bytes 811016 | tf_op jit(solution)/shard_map/ppermute | solution.py:29
  520.8 8.6 collective-permute-start.22
  522.7 8.6 collective-permute-start.23
  532.1 1.0 copy-start.6
  535.0 3.5 collective-permute-start.24
  537.2 4.9 collective-permute-start.25
  542.1 7.2 collective-permute-start.26
  544.1 7.2 collective-permute-start.27
  552.0 4.5 collective-permute-start.28
  555.2 5.3 collective-permute-start.29
  561.2 7.4 collective-permute-start.30
  563.1 7.2 collective-permute-start.31
  571.0 67.2 %copy-start.18 = (f32[2,64,512]{2,1,0:T(8,128)}, f32[2,64,512]{2,1,0:T(8,128)S(1)}, u32[]{:S(2)}) copy-start(f32[2,64,512]{2,1,0:T(8,128)S(1)} %div.91) | copy-start | bytes 786436
  571.8 385.9 %reduce-scatter.2.cloned.1.call-start = ((), (), s32[]{:S(2)}) async-start(), calls=%async_computation.3 | async-start | bytes 1056768 | tf_op jit(solution)/shard_map/reduce_scatter | solution.py:174
  638.2 54.6 %copy-start.19 = (f32[1,256,128]{2,1,0:T(8,128)S(1)}, f32[1,256,128]{2,1,0:T(8,128)}, u32[]{:S(2)}) copy-start(f32[1,256,128]{2,1,0:T(8,128)} %param.27) | copy-start | bytes 393220
  638.2 54.6 %copy-start.20 = (f32[256,128]{1,0:T(8,128)S(1)}, f32[256,128]{1,0:T(8,128)}, u32[]{:S(2)}) copy-start(f32[256,128]{1,0:T(8,128)} %get-tuple-element.135) | copy-start | bytes 393220
  (8 other events, 6.6 us)
Sparse Core Ops, SparseCore 0:
  571.9 66.2 all-reduce.9
  695.5 262.1 reduce-scatter.1
